TPU v7x, 128 devices: a whole 4x4x4 slice. The times are simulated.
128 devices in a mesh: dp: 2 (over x_lo), seq: 16 (over z, y), mp: 4 (over x_hi, core).
Axes of the slice: x: 4 (x_hi: 2, x_lo: 2; x = x_hi * 2 + x_lo), y: 4, z: 4, core: 2. Of those that a mesh axis runs over, the one named last changes fastest.
Arguments:
- shortening_input: bfloat16 [2, 32768, 2048], P('dp', ('seq', 'mp')), may hold values from -16 to 16
- coarse_grad: bfloat16 [2, 8192, 4096], P('dp', 'seq', 'mp'), may hold values from -6 to 6
- weight_copy: bfloat16 [2, 4096, 4096], P('dp', None, 'mp'), may hold values from -0.0625 to 0.0625
- master: float32 [2, 4096, 4096], P('dp', 'seq', 'mp'), may hold values from -3 to 3
- moment: float32 [2, 4096, 4096], P('dp', 'seq', 'mp'), may hold values from -3 to 3
- second: float32 [2, 4096, 4096], P('dp', 'seq', 'mp'), may hold values from 0.05 to 5
Outputs:
- act_grad: bfloat16 [2, 32768, 2048], P('dp', ('seq', 'mp'))
- new_master: float32 [2, 4096, 4096], P('dp', 'seq', 'mp')
- new_moment: float32 [2, 4096, 4096], P('dp', 'seq', 'mp')
- new_second: float32 [2, 4096, 4096], P('dp', 'seq', 'mp')
- new_weight: bfloat16 [2, 4096, 4096], P(None, 'seq', 'mp')
All inputs are finite; a program needn't handle non-finite values.
Results may differ from a plain program's by a relative error of at most 0.009.
Values may be sent and summed in bfloat16 or wider, within the bound.
A program may use at most 128 MiB of HBM per device.

v0:
```python
import math
import jax
import jax.numpy as jnp
from jax import lax
from jax.sharding import PartitionSpec as P

SHORT = 4
first_beta = 0.9
second_beta = 0.95
first_fix = 1.0 - 0.9**10
second_fix = 1.0 - 0.95**10
adam_eps = 1e-08
learn_rate = 0.05
weight_decay = 0.1


def shifted(value, axis, steps):
    count = lax.axis_size(axis)
    initial, last = (max(0, -steps), min(count, count - steps))
    return lax.ppermute(value, axis, [(source, source + steps) for source in range(initial, last)])


def per_device(shortening_input, coarse_grad, weight_copy, master, moment, second):
    fine_rows = shortening_input[0]
    rows_dev = fine_rows.shape[0]
    features = fine_rows.shape[1]
    grad_cols = coarse_grad[0]
    coarse_rows = grad_cols.shape[0]
    wide_rows = SHORT * features
    whole_copy = lax.all_gather(weight_copy, "dp", axis=0, tiled=True)
    weights = whole_copy.reshape(wide_rows, whole_copy.shape[2])
    summed = (
        lax.psum_scatter(
            lax.dot_general(
                grad_cols, weights, (((1,), (1,)), ((), ())), preferred_element_type=jnp.float32
            ).astype(jnp.bfloat16),
            "mp",
            scatter_dimension=0,
            tiled=True,
        )
        .astype(jnp.float32)
        .reshape(rows_dev, features)
    )
    later_rows = shifted(summed[: SHORT - 1], ("seq", "mp"), -1)
    act_grad = jnp.concatenate([summed[SHORT - 1 :], later_rows], axis=0).astype(jnp.bfloat16)
    gathered = lax.all_gather(fine_rows, "mp", axis=0, tiled=True).reshape(coarse_rows, wide_rows)
    owned_rows = lax.psum_scatter(
        lax.dot_general(
            gathered, grad_cols, (((0,), (0,)), ((), ())), preferred_element_type=jnp.float32
        ).astype(jnp.bfloat16),
        ("dp", "seq"),
        scatter_dimension=0,
        tiled=True,
    ).astype(jnp.float32)
    grad_scale = 1.0 / math.sqrt(lax.axis_size("dp") * coarse_rows * lax.axis_size("seq"))
    gradient = (owned_rows * grad_scale).reshape(master.shape)
    new_moment = first_beta * moment + (1.0 - first_beta) * gradient
    new_second = second_beta * second + (1.0 - second_beta) * gradient * gradient
    step_ratio = new_moment / first_fix / (jnp.sqrt(new_second / second_fix) + adam_eps)
    new_master = master - learn_rate * (step_ratio + weight_decay * master)
    new_weight = lax.all_gather(new_master.astype(jnp.bfloat16), "dp", axis=0, tiled=True)
    return (act_grad[None], new_master, new_moment, new_second, new_weight)


def solution(mesh):
    return jax.shard_map(
        per_device,
        mesh=mesh,
        in_specs=(
            P("dp", ("seq", "mp"), None),
            P("dp", "seq", "mp"),
            P("dp", None, "mp"),
            P("dp", "seq", "mp"),
            P("dp", "seq", "mp"),
            P("dp", "seq", "mp"),
        ),
        out_specs=(
            P("dp", ("seq", "mp"), None),
            P("dp", "seq", "mp"),
            P("dp", "seq", "mp"),
            P("dp", "seq", "mp"),
            P(None, "seq", "mp"),
        ),
        check_vma=False,
    )
```

profile of v0, /device:TPU:1, one launch (start us, length us, event | category | flops | bytes accessed | tf_op | source)
XLA Modules:
  0.0 598.7 jit_solution(8087881129983664939)
XLA Ops:
  7.2 0.0 all-gather.9.cloned.1.call-start
  7.2 0.7 all-gather.9.cloned.1.call-update
  7.9 0.0 all-gather.5.cloned.1.call-start
  8.0 0.7 all-gather.5.cloned.1.call-update
  8.7 0.0 reduce-scatter.5.cloned.1.call-start
  8.7 66.9 %all-gather.9.cloned.1.call-done = bf16[1,2048,2048]{2,1,0:T(8,128)(2,1)} async-done(((bf16[1,512,2048]{2,1,0:T(8,128)(2,1)}), bf16[1,2048,2048]{2,1,0:T(8,128)(2,1)}) %all-gather.9.cloned.1.call-update) | async-done | bytes 8388624 | tf_op jit(solution)/shard_map/all_gather | solution.py:46
  75.6 15.1 %reshape.57 = bf16[512,8192]{1,0:T(8,128)(2,1)} reshape(bf16[1,2048,2048]{2,1,0:T(8,128)(2,1)} %all-gather.9.cloned.1.call-done) | data formatting | bytes 16777216 | tf_op jit(solution)/shard_map/reshape | solution.py:46
  90.7 17.8 %convolution_convert_fusion = bf16[8192,1024]{1,0:T(8,128)(2,1)} fusion(bf16[512,8192]{1,0:T(8,128)(2,1)} %reshape.57, bf16[1,512,1024]{2,1,0:T(8,128)(2,1)S(1)} %copy-done), kind=kOutput, calls=%fused_computation | convolution fusion | flops 8598323200 | bytes 26214400 | tf_op jit(solution)/shard_map/dot_general | solution.py:48
  108.4 0.0 reduce-scatter.5.cloned.1.call-update
  108.4 0.0 reduce-scatter.3.cloned.1.call-start
  108.5 169.0 %all-gather.5.cloned.1.call-done = bf16[2,4096,1024]{2,1,0:T(8,128)(2,1)} async-done(((bf16[1,4096,1024]{2,1,0:T(8,128)(2,1)}), bf16[2,4096,1024]{2,1,0:T(8,128)(2,1)}) %all-gather.5.cloned.1.call-update) | async-done | bytes 16777232 | tf_op jit(solution)/shard_map/all_gather | solution.py:30
  277.5 29.6 %convolution_convert_fusion.1 = bf16[512,8192]{1,0:T(8,128)(2,1)} fusion(bf16[8192,1024]{1,0:T(8,128)(2,1)} %bitcast.24, bf16[1,512,1024]{2,1,0:T(8,128)(2,1)S(1)} %copy-done), kind=kOutput, calls=%fused_computation.1 | convolution fusion | flops 8594128896 | bytes 26214400 | tf_op jit(solution)/shard_map/dot_general | solution.py:34
  307.1 0.0 reduce-scatter.3.cloned.1.call-update
  307.1 0.0 all-gather.7.cloned.1.call-start
  307.2 160.9 %reduce-scatter.5.cloned.1.call-done = bf16[256,1024]{1,0:T(8,128)(2,1)} async-done(((bf16[8192,1024]{1,0:T(8,128)(2,1)}), bf16[256,1024]{1,0:T(8,128)(2,1)}) %reduce-scatter.5.cloned.1.call-update) | async-done | bytes 524304 | tf_op jit(solution)/shard_map/reduce_scatter | solution.py:47
  468.1 3.9 fusion.7
  472.0 92.6 %reduce-scatter.3.cloned.1.call-done = bf16[128,8192]{1,0:T(8,128)(2,1)} async-done(((bf16[512,8192]{1,0:T(8,128)(2,1)}), bf16[128,8192]{1,0:T(8,128)(2,1)}) %reduce-scatter.3.cloned.1.call-update) | async-done | bytes 2097168 | tf_op jit(solution)/shard_map/reduce_scatter | solution.py:33
  564.5 3.4 reshape.56
  567.9 2.7 collective-permute-start
  570.7 0.5 slice_bitcast_fusion
  571.2 3.3 collective-permute-done
  574.5 1.5 pad_maximum_fusion
  576.0 13.9 %all-gather.7.cloned.1.call-done = bf16[2,256,1024]{2,1,0:T(8,128)(2,1)} async-done(((bf16[1,256,1024]{2,1,0:T(8,128)(2,1)}), bf16[2,256,1024]{2,1,0:T(8,128)(2,1)}) %all-gather.7.cloned.1.call-update) | async-done | bytes 1048592 | tf_op jit(solution)/shard_map/all_gather | solution.py:61
  589.9 2.3 copy.12
  (10 shorter events, 0.0 us)
Async XLA Ops:
  7.2 83.5 %copy-start = (bf16[1,512,1024]{2,1,0:T(8,128)(2,1)S(1)}, bf16[1,512,1024]{2,1,0:T(8,128)(2,1)}, u32[]{:S(2)}) copy-start(bf16[1,512,1024]{2,1,0:T(8,128)(2,1)} %param.7) | copy-start | bytes 3145732
  7.2 68.4 %all-gather.9.cloned.1.call-start = ((), (), s32[]{:S(2)}) async-start(), calls=%async_computation.6 | async-start | bytes 10485760 | tf_op jit(solution)/shard_map/all_gather | solution.py:46
  7.9 269.6 %all-gather.5.cloned.1.call-start = ((), (), s32[]{:S(2)}) async-start(), calls=%async_computation.2 | async-start | bytes 25165824 | tf_op jit(solution)/shard_map/all_gather | solution.py:30
  8.7 459.4 %reduce-scatter.5.cloned.1.call-start = ((), (), s32[]{:S(2)}) async-start(), calls=%async_computation.4 | async-start | bytes 17301504 | tf_op jit(solution)/shard_map/reduce_scatter | solution.py:47
  108.4 456.1 %reduce-scatter.3.cloned.1.call-start = ((), (), s32[]{:S(2)}) async-start(), calls=%async_computation.3 | async-start | bytes 10485760 | tf_op jit(solution)/shard_map/reduce_scatter | solution.py:33
  307.1 161.0 %copy-start.2 = (f32[1,256,1024]{2,1,0:T(8,128)S(1)}, f32[1,256,1024]{2,1,0:T(8,128)}, u32[]{:S(2)}) copy-start(f32[1,256,1024]{2,1,0:T(8,128)} %param.9) | copy-start | bytes 3145732
  307.1 161.0 %copy-start.3 = (f32[1,256,1024]{2,1,0:T(8,128)S(1)}, f32[1,256,1024]{2,1,0:T(8,128)}, u32[]{:S(2)}) copy-start(f32[1,256,1024]{2,1,0:T(8,128)} %param.10) | copy-start | bytes 3145732
  307.1 282.8 %all-gather.7.cloned.1.call-start = ((), (), s32[]{:S(2)}) async-start(), calls=%async_computation.5 | async-start | bytes 1572864 | tf_op jit(solution)/shard_map/all_gather | solution.py:61
  468.1 124.1 %copy-start.1 = (bf16[1,512,1024]{2,1,0:T(8,128)(2,1)S(1)}, bf16[1,512,1024]{2,1,0:T(8,128)(2,1)}, u32[]{:S(2)}) copy-start(bf16[1,512,1024]{2,1,0:T(8,128)(2,1)} %param.7) | copy-start | bytes 3145732
  567.9 6.6 %collective-permute-start = (bf16[3,2048]{1,0:T(4,128)(2,1)S(1)}, bf16[3,2048]{1,0:T(4,128)(2,1)S(1)}, u32[]{:S(2)}, u32[]{:S(2)}) collective-permute-start(bf16[3,2048]{1,0:T(4,128)(2,1)S(1)} %slice.18), channel_id=1, source_target_pairs={{1,0},{2,1},{3,2},{4,3},{5,4},{6,5},{7,6},{8,7},{9,8},{10,9},{11,1... | collective-permute-start | bytes 36872 | tf_op jit(solution)/shard_map/ppermute | solution.py:20
Sparse Core Ops, SparseCore 0:
  9.7 65.8 all-gather.8
  77.2 200.2 all-gather.4
  279.9 188.1 reduce-scatter.4
  470.6 93.8 reduce-scatter.2
  566.6 23.2 all-gather.6
where the time goes:
time: 599 us
  waiting for transfers between devices  508 us (85%)
  matrix products  47.4 us (8%)
  local copies, waits for them, and re-layouts  21.2 us (4%)
  between operations  13.8 us (2%)
    all_gather x1, waiting for transfers between devices, per_device(): whole_copy = lax.all_gather(weight_copy, 'dp', axis=0, tiled=True)  169 us
    reduce_scatter x1, waiting for transfers between devices, per_device(): lax.psum_scatter(lax.dot_general(gathered, grad_cols, (((0,), (0,)), ((),...  161 us
    reduce_scatter x1, waiting for transfers between devices, per_device(): lax.psum_scatter(lax.dot_general(grad_cols, weights, (((1,), (1,)), ((),...  92.6 us
    all_gather x1, waiting for transfers between devices, per_device(): lax.all_gather(fine_rows, 'mp', axis=0, tiled=True)  66.9 us
    dot_general x1, matrix products, per_device(): lax.dot_general(grad_cols, weights, (((1,), (1,)), ((), ())), preferred_e...  29.6 us
    dot_general x1, matrix products, per_device(): lax.dot_general(gathered, grad_cols, (((0,), (0,)), ((), ())), preferred_...  17.8 us
    reshape x1, local copies, waits for them, and re-layouts, per_device(): lax.all_gather(fine_rows, 'mp', axis=0, tiled=True)  15.1 us
    all_gather x1, waiting for transfers between devices, per_device(): lax.all_gather(new_master.astype(jnp.bfloat16), 'dp', axis=0, tiled=True)  13.9 us
  transfers between devices with their start and end apart: 6, of which 6 were waited for; matrix products, arithmetic and copies ran while one was open for 12% of the time, Pallas kernels for 0%

commit v1 on v0

--- a/solution.py
+++ b/solution.py
@@ -43,7 +43,11 @@
     )
     later_rows = shifted(summed[: SHORT - 1], ("seq", "mp"), -1)
     act_grad = jnp.concatenate([summed[SHORT - 1 :], later_rows], axis=0).astype(jnp.bfloat16)
-    gathered = lax.all_gather(fine_rows, "mp", axis=0, tiled=True).reshape(coarse_rows, wide_rows)
+    handle_the_axis_part = lambda patch, across: jnp.concatenate(
+        lax.all_to_all(jnp.stack([patch for _ in range(lax.axis_size(across))]), across, 0, 0),
+        axis=0,
+    )
+    gathered = handle_the_axis_part(fine_rows, "mp").reshape(coarse_rows, wide_rows)
     owned_rows = lax.psum_scatter(
         lax.dot_general(
             gathered, grad_cols, (((0,), (0,)), ((), ())), preferred_element_type=jnp.float32

time: 599 us -> 585 us (0.977)
  waiting for transfers between devices: 508 us -> 319 us
  blocking collectives: 0 us -> 173 us
    all_to_all x0 -> x1, blocking collectives: none -> 173 us  [per_device(): lax.all_to_all(jnp.stack([patch for _ in range(lax.axis_size(across))]),...]
    all_gather x1, waiting for transfers between devices: 169 us -> 74.1 us  [per_device(): whole_copy = lax.all_gather(weight_copy, 'dp', axis=0, tiled=True)]
    all_gather x1 -> x0, waiting for transfers between devices: 66.9 us -> none  [per_device(): lax.all_gather(fine_rows, 'mp', axis=0, tiled=True)]
    another operation x0 -> x2, local copies, waits for them, and re-layouts: none -> 15.7 us  [the longest x1 14.6 us: per_device(): handle_the_axis_part(fine_rows, 'mp').reshape(coarse_rows, wide_rows)]
    reshape x1 -> x0, local copies, waits for them, and re-layouts: 15.1 us -> none  [per_device(): lax.all_gather(fine_rows, 'mp', axis=0, tiled=True)]
    all_gather x1, waiting for transfers between devices: 13.9 us -> 0.01 us  [per_device(): lax.all_gather(new_master.astype(jnp.bfloat16), 'dp', axis=0, tiled=True)]
    reduce_scatter x1, waiting for transfers between devices: 161 us -> 148 us  [per_device(): lax.psum_scatter(lax.dot_general(gathered, grad_cols, (((0,), (0,)), ((),...]
  transfers between devices with their start and end apart: 6 -> 5, of which waited for: 6 -> 4; matrix products, arithmetic and copies ran while one was open for 12% -> 12% of each run, Pallas kernels for 0% -> 0%
where the time goes in v1:
time: 585 us; the launch traced here: 584 us
  waiting for transfers between devices  319 us (55%)
  blocking collectives  173 us (30%)
  matrix products  45.6 us (8%)
  local copies, waits for them, and re-layouts  22.8 us (4%)
  between operations  15.6 us (3%)
    all_to_all x1, blocking collectives, per_device(): lax.all_to_all(jnp.stack([patch for _ in range(lax.axis_size(across))]),...  173 us
    reduce_scatter x1, waiting for transfers between devices, per_device(): lax.psum_scatter(lax.dot_general(gathered, grad_cols, (((0,), (0,)), ((),...  148 us
    reduce_scatter x1, waiting for transfers between devices, per_device(): lax.psum_scatter(lax.dot_general(grad_cols, weights, (((1,), (1,)), ((),...  93.4 us
    all_gather x1, waiting for transfers between devices, per_device(): whole_copy = lax.all_gather(weight_copy, 'dp', axis=0, tiled=True)  74.1 us
    dot_general x1, matrix products, per_device(): lax.dot_general(grad_cols, weights, (((1,), (1,)), ((), ())), preferred_e...  29.6 us
    dot_general x1, matrix products, per_device(): lax.dot_general(gathered, grad_cols, (((0,), (0,)), ((), ())), preferred_...  15.9 us
    another operation x1, local copies, waits for them, and re-layouts, per_device(): handle_the_axis_part(fine_rows, 'mp').reshape(coarse_rows, wide_rows)  14.6 us
  transfers between devices with their start and end apart: 5, of which 4 were waited for; matrix products, arithmetic and copies ran while one was open for 12% of the time, Pallas kernels for 0%

profile of v1, /device:TPU:1, one launch (start us, length us, event | category | flops | bytes accessed | tf_op | source)
XLA Modules:
  0.0 584.2 jit_solution(17745096046316756937)
XLA Ops:
  8.0 0.0 all-gather.3.cloned.1.call-start
  8.1 0.7 all-gather.3.cloned.1.call-update
  8.8 0.0 reduce-scatter.5.cloned.1.call-start
  8.8 0.9 copy-done.2
  9.7 1.1 stack.3
  10.8 172.8 %all_to_all.5 = bf16[4,512,2048]{2,1,0:T(8,128)(2,1)} all-to-all(bf16[4,512,2048]{2,1,0:T(8,128)(2,1)S(1)} %stack.3), channel_id=1, replica_groups=mesh['dp'=2,'seq'=16,'mp'=4] {'mp'}, dimensions={0} | all-to-all | bytes 16777216 | tf_op jit(solution)/shard_map/all_to_all | solution.py:47
  183.6 14.6 %reshape_reshape.3 = bf16[512,8192]{1,0:T(8,128)(2,1)} reshape(bf16[4,512,2048]{2,1,0:T(8,128)(2,1)} %all_to_all.5) | data formatting | bytes 16777216 | tf_op jit(solution)/shard_map/reshape;reshape | solution.py:50
  198.2 15.9 %convolution_convert_fusion = bf16[8192,1024]{1,0:T(8,128)(2,1)} fusion(bf16[512,8192]{1,0:T(8,128)(2,1)} %reshape_reshape.3, bf16[1,512,1024]{2,1,0:T(8,128)(2,1)S(1)} %copy-done), kind=kOutput, calls=%fused_computation | convolution fusion | flops 8598323200 | bytes 26214400 | tf_op jit(solution)/shard_map/dot_general | solution.py:52
  214.1 0.0 reduce-scatter.5.cloned.1.call-update
  214.1 0.0 reduce-scatter.3.cloned.1.call-start
  214.2 74.1 %all-gather.3.cloned.1.call-done = bf16[2,4096,1024]{2,1,0:T(8,128)(2,1)} async-done(((bf16[1,4096,1024]{2,1,0:T(8,128)(2,1)}), bf16[2,4096,1024]{2,1,0:T(8,128)(2,1)}) %all-gather.3.cloned.1.call-update) | async-done | bytes 16777232 | tf_op jit(solution)/shard_map/all_gather | solution.py:30
  288.3 29.6 %convolution_convert_fusion.1 = bf16[512,8192]{1,0:T(8,128)(2,1)} fusion(bf16[8192,1024]{1,0:T(8,128)(2,1)} %bitcast.26, bf16[1,512,1024]{2,1,0:T(8,128)(2,1)S(1)} %copy-done), kind=kOutput, calls=%fused_computation.1 | convolution fusion | flops 8594128896 | bytes 26214400 | tf_op jit(solution)/shard_map/dot_general | solution.py:34
  318.0 0.0 reduce-scatter.3.cloned.1.call-update
  318.0 0.0 all-gather.5.cloned.1.call-start
  318.0 147.7 %reduce-scatter.5.cloned.1.call-done = bf16[256,1024]{1,0:T(8,128)(2,1)} async-done(((bf16[8192,1024]{1,0:T(8,128)(2,1)}), bf16[256,1024]{1,0:T(8,128)(2,1)}) %reduce-scatter.5.cloned.1.call-update) | async-done | bytes 524304 | tf_op jit(solution)/shard_map/reduce_scatter | solution.py:51
  465.8 3.9 fusion.7
  469.7 0.0 all-gather.5.cloned.1.call-update
  469.7 93.4 %reduce-scatter.3.cloned.1.call-done = bf16[128,8192]{1,0:T(8,128)(2,1)} async-done(((bf16[512,8192]{1,0:T(8,128)(2,1)}), bf16[128,8192]{1,0:T(8,128)(2,1)}) %reduce-scatter.3.cloned.1.call-update) | async-done | bytes 2097168 | tf_op jit(solution)/shard_map/reduce_scatter | solution.py:33
  563.1 3.4 reshape.54
  566.5 2.8 collective-permute-start
  569.3 0.5 slice_bitcast_fusion
  569.8 3.2 collective-permute-done
  573.0 1.5 pad_maximum_fusion
  574.5 2.3 copy.12
  (11 shorter events, 0.0 us)
Async XLA Ops:
  8.0 190.2 %copy-start = (bf16[1,512,1024]{2,1,0:T(8,128)(2,1)S(1)}, bf16[1,512,1024]{2,1,0:T(8,128)(2,1)}, u32[]{:S(2)}) copy-start(bf16[1,512,1024]{2,1,0:T(8,128)(2,1)} %param.7) | copy-start | bytes 3145732
  8.0 1.7 copy-start.2
  8.0 280.3 %all-gather.3.cloned.1.call-start = ((), (), s32[]{:S(2)}) async-start(), calls=%async_computation.3 | async-start | bytes 25165824 | tf_op jit(solution)/shard_map/all_gather | solution.py:30
  8.8 457.0 %reduce-scatter.5.cloned.1.call-start = ((), (), s32[]{:S(2)}) async-start(), calls=%async_computation.5 | async-start | bytes 17301504 | tf_op jit(solution)/shard_map/reduce_scatter | solution.py:51
  214.1 348.9 %reduce-scatter.3.cloned.1.call-start = ((), (), s32[]{:S(2)}) async-start(), calls=%async_computation.4 | async-start | bytes 10485760 | tf_op jit(solution)/shard_map/reduce_scatter | solution.py:33
  318.0 147.8 %copy-start.3 = (f32[1,256,1024]{2,1,0:T(8,128)S(1)}, f32[1,256,1024]{2,1,0:T(8,128)}, u32[]{:S(2)}) copy-start(f32[1,256,1024]{2,1,0:T(8,128)} %param.9) | copy-start | bytes 3145732
  318.0 147.8 %copy-start.4 = (f32[1,256,1024]{2,1,0:T(8,128)S(1)}, f32[1,256,1024]{2,1,0:T(8,128)}, u32[]{:S(2)}) copy-start(f32[1,256,1024]{2,1,0:T(8,128)} %param.10) | copy-start | bytes 3145732
  318.0 256.5 %all-gather.5.cloned.1.call-start = ((), (), s32[]{:S(2)}) async-start(), calls=%async_computation.6 | async-start | bytes 1572864 | tf_op jit(solution)/shard_map/all_gather | solution.py:65
  465.8 111.0 %copy-start.1 = (bf16[1,512,1024]{2,1,0:T(8,128)(2,1)S(1)}, bf16[1,512,1024]{2,1,0:T(8,128)(2,1)}, u32[]{:S(2)}) copy-start(bf16[1,512,1024]{2,1,0:T(8,128)(2,1)} %param.7) | copy-start | bytes 3145732
  566.5 6.6 %collective-permute-start = (bf16[3,2048]{1,0:T(4,128)(2,1)S(1)}, bf16[3,2048]{1,0:T(4,128)(2,1)S(1)}, u32[]{:S(2)}, u32[]{:S(2)}) collective-permute-start(bf16[3,2048]{1,0:T(4,128)(2,1)S(1)} %slice.18), channel_id=1, source_target_pairs={{1,0},{2,1},{3,2},{4,3},{5,4},{6,5},{7,6},{8,7},{9,8},{10,9},{11,1... | collective-permute-start | bytes 36872 | tf_op jit(solution)/shard_map/ppermute | solution.py:20
Sparse Core Ops, SparseCore 0:
  10.5 277.7 all-gather.2
  469.8 40.4 all-gather.4
Sparse Core Ops, SparseCore 1:
  214.2 251.5 reduce-scatter.4
  468.3 94.7 reduce-scatter.2
